TPU v7x, 256 devices: a whole 4x4x8 slice. The times are simulated.
256 devices in a mesh: row: 32 (over z, y_lo, core), col: 8 (over y_hi, x).
Axes of the slice: x: 4, y: 4 (y_hi: 2, y_lo: 2; y = y_hi * 2 + y_lo), z: 8, core: 2. Of those that a mesh axis runs over, the one named last changes fastest.
Arguments:
- matrix: float32 [14336, 14336], P('row', 'col'), may hold values from -16 to 16, as said below
- panels: float32 [2, 14336, 128], P(None, 'row'), may hold values from -0.050111484 to 0.050111484
- factors: float32 [2, 128, 128], replicated, may hold values from -1.2 to 1.6, as said below
Outputs:
- updated: float32 [14336, 14336], P('row', 'col')
Inputs may be any that keep to these rules, and one draw needn't show every extreme that they name: symmetric: matrix[r, c] equals matrix[c, r]. Each factors[p] is upper triangular, with diagonal entries between 0.8 and 1.6.
All inputs are finite; a program needn't handle non-finite values.
Results may differ from a plain program's by a relative error of at most 0.0001.
Values sent between devices are 32-bit elements; how exact they have to be, the bound alone decides.
A program may use at most 64 MiB of HBM per device.

v0:
```python
import jax
import jax.numpy as jnp
from jax import lax
from jax.sharding import PartitionSpec as P


def matmul(former, latter):
    return jnp.dot(former, latter, precision=lax.Precision.HIGHEST)


def transposed_dot(former, latter):
    return lax.dot_general(
        former, latter, (((0,), (0,)), ((), ())), precision=lax.Precision.HIGHEST
    )


def outer_drop(current, former, latter):
    return current - lax.dot_general(
        former, latter, (((1,), (1,)), ((), ())), precision=lax.Precision.HIGHEST
    )


def weights(forward, vectors, factor, correct):
    return matmul(forward, factor) - 0.5 * matmul(vectors, correct)


def row_sums(current, vector_rows, extra_terms):
    summed = lax.psum((transposed_dot(current, vector_rows),) + extra_terms, "row")
    return (summed[0], tuple(summed[1:]))


def shards(matrix, panels, factors):
    col_index = lax.axis_index("col")
    local_cols = matrix.shape[1]
    gathered = lax.all_gather(panels, "row", axis=1, tiled=True)
    vector_cols = lax.dynamic_slice_in_dim(gathered, col_index * local_cols, local_cols, 1)
    current = matrix
    for number in range(panels.shape[0]):
        vector_rows = panels[number]
        vcol_now = vector_cols[number]
        factor = factors[number]
        forward = lax.psum(matmul(current, vcol_now), "col")
        forward_cols, summed = row_sums(
            current, vector_rows, (transposed_dot(vector_rows, forward),)
        )
        correct = matmul(factor.T, matmul(summed[0], factor))
        wrow_now = weights(forward, vector_rows, factor, correct)
        wcol_now = weights(forward_cols, vcol_now, factor, correct)
        current = outer_drop(
            current,
            jnp.concatenate([vector_rows, wrow_now], axis=1),
            jnp.concatenate([wcol_now, vcol_now], axis=1),
        )
    return current


def solution(mesh):
    placed = (P("row", "col"), P(None, "row", None), P())
    return jax.shard_map(
        shards, mesh=mesh, in_specs=placed, out_specs=P("row", "col"), check_vma=False
    )
```

profile of v0, /device:TPU:1, one launch (start us, length us, event | category | flops | bytes accessed | tf_op | source)
XLA Modules:
  0.0 775.0 jit_solution(1958344349460214117)
XLA Ops:
  6.5 0.0 copy-start
  6.5 0.0 all-gather.2.cloned.1.call-start
  6.5 0.7 all-gather.2.cloned.1.call-update
  7.3 0.0 all-reduce.7.cloned.1.call-start
  7.3 95.2 %all-gather.2.cloned.1.call-done = f32[2,14336,128]{2,1,0:T(8,128)} async-done(((f32[2,448,128]{2,1,0:T(8,128)}), f32[2,14336,128]{2,1,0:T(8,128)}) %all-gather.2.cloned.1.call-update) | async-done | bytes 14680080 | tf_op jit(solution)/shard_map/all_gather | solution.py:35
  102.5 2.5 dynamic-slice_bitcast_fusion
  105.0 0.0 copy-start.3
  105.0 0.9 copy-done.3
  105.9 0.0 copy-done
  105.9 3.4 convolution_bitcast_fusion
  109.3 0.0 all-reduce.7.cloned.1.call-update
  109.3 0.0 copy-start.7
  109.3 0.0 all-reduce.13.cloned.1.call-start
  109.4 7.8 %fusion.44 = f32[1792,128]{1,0:T(8,128)} fusion(f32[448,1792]{1,0:T(8,128)S(1)} %copy-done, f32[2,448,128]{2,1,0:T(8,128)} %param.4), kind=kOutput, calls=%fused_computation.57 | convolution fusion | flops 1233125376 | bytes 4358144 | tf_op jit(solution)/shard_map/dot_general | solution.py:12
  117.2 0.0 copy-start.4
  117.2 74.7 %all-reduce.7.cloned.1.call-done = f32[448,128]{1,0:T(8,128)} async-done(((f32[448,128]{1,0:T(8,128)}), f32[448,128]{1,0:T(8,128)}) %all-reduce.7.cloned.1.call-update) | async-done | bytes 229392 | tf_op jit(solution)/shard_map/psum | solution.py:42
  191.9 2.3 convolution_bitcast_fusion.2
  194.1 0.0 all-reduce.13.cloned.1.call-update
  194.2 0.0 copy-start.5
  194.2 0.2 all-reduce.9.cloned.1.call-start
  194.4 1.9 slice_bitcast_fusion
  196.3 0.0 copy-done.7
  196.3 1.3 fusion.32
  197.6 228.8 %all-reduce.13.cloned.1.call-done = (f32[1792,128]{1,0:T(8,128)}, f32[128,128]{0,1:T(8,128)}) async-done(((f32[1792,128]{1,0:T(8,128)}, f32[128,128]{0,1:T(8,128)}), (f32[1792,128]{1,0:T(8,128)}, f32[128,128]{0,1:T(8,128)})) %all-reduce.13.cloned.1.call-update) | async-done | bytes 983056 | tf_op jit(solution)/shard_map/psum | solution.py:28
  426.3 0.0 copy-start.9
  426.3 2.1 fusion.26
  428.4 1.1 fusion.30
  429.6 0.3 fusion.28
  429.9 0.0 copy-done.4
  429.9 0.9 fusion.1
  430.8 0.0 copy-done.5
  430.8 0.4 fusion.11
  431.1 0.0 copy-done.9
  431.2 0.0 copy-start.1
  431.2 5.1 convolution_subtract_fusion.1
  436.3 0.0 copy-done.1
  436.3 3.4 fusion.46
  439.6 0.0 all-reduce.9.cloned.1.call-update
  439.7 0.3 all-reduce.11.cloned.1.call-start
  439.9 7.8 %fusion.45 = f32[1792,128]{1,0:T(8,128)} fusion(f32[448,1792]{1,0:T(8,128)S(1)} %convolution_subtract_fusion.1, f32[2,448,128]{2,1,0:T(8,128)} %param.4), kind=kOutput, calls=%fused_computation.58 | convolution fusion | flops 1233125376 | bytes 4358144 | tf_op jit(solution)/shard_map/dot_general | solution.py:12
  447.7 75.9 %all-reduce.9.cloned.1.call-done = f32[448,128]{1,0:T(8,128)} async-done(((f32[448,128]{1,0:T(8,128)}), f32[448,128]{1,0:T(8,128)}) %all-reduce.9.cloned.1.call-update) | async-done | bytes 229392 | tf_op jit(solution)/shard_map/psum | solution.py:42
  523.6 2.3 convolution_bitcast_fusion.1
  525.9 0.0 all-reduce.11.cloned.1.call-update
  525.9 2.0 fusion.24
  527.9 230.0 %all-reduce.11.cloned.1.call-done = (f32[1792,128]{1,0:T(8,128)}, f32[128,128]{0,1:T(8,128)}) async-done(((f32[1792,128]{1,0:T(8,128)}, f32[128,128]{0,1:T(8,128)}), (f32[1792,128]{1,0:T(8,128)}, f32[128,128]{0,1:T(8,128)})) %all-reduce.11.cloned.1.call-update) | async-done | bytes 983056 | tf_op jit(solution)/shard_map/psum | solution.py:28
  757.9 0.0 copy-start.6
  757.9 0.0 copy-start.10
  757.9 0.0 copy-start.2
  757.9 0.0 copy-start.8
  757.9 2.2 fusion.18
  760.1 1.1 fusion.22
  761.2 0.3 fusion.20
  761.5 2.1 fusion
  763.6 0.0 copy-done.6
  763.6 0.0 copy-done.10
  763.6 0.4 fusion.9
  764.0 0.0 copy-done.2
  764.0 0.0 copy-done.8
  764.0 4.5 convolution_subtract_fusion
Async XLA Ops:
  6.5 99.4 %copy-start = (f32[448,1792]{1,0:T(8,128)S(1)}, f32[448,1792]{1,0:T(8,128)}, u32[]{:S(2)}) copy-start(f32[448,1792]{1,0:T(8,128)} %param.3) | copy-start | bytes 9633796
  6.5 96.0 %all-gather.2.cloned.1.call-start = ((), (), s32[]{:S(2)}) async-start(), calls=%async_computation | async-start | bytes 15138816 | tf_op jit(solution)/shard_map/all_gather | solution.py:35
  7.3 184.6 %all-reduce.7.cloned.1.call-start = ((), (), s32[]{:S(2)}) async-start(), calls=%async_computation.1 | async-start | bytes 458752 | tf_op jit(solution)/shard_map/psum | solution.py:42
  105.0 0.9 copy-start.3
  109.3 87.0 %copy-start.7 = (f32[2,128,128]{2,1,0:T(8,128)S(1)}, f32[2,128,128]{2,1,0:T(8,128)}, u32[]{:S(2)}) copy-start(f32[2,128,128]{2,1,0:T(8,128)} %param.5) | copy-start | bytes 393220
  109.3 317.0 %all-reduce.13.cloned.1.call-start = ((), (), s32[]{:S(2)}) async-start(), calls=%async_computation.4 | async-start | bytes 1966080 | tf_op jit(solution)/shard_map/psum | solution.py:28
  117.2 312.7 %copy-start.4 = (f32[1792,128]{1,0:T(8,128)S(1)}, f32[1792,128]{1,0:T(8,128)}, u32[]{:S(2)}) copy-start(f32[1792,128]{1,0:T(8,128)} %copy-done.3) | copy-start | bytes 2752516
  194.2 236.6 %copy-start.5 = (f32[2,448,128]{2,1,0:T(8,128)S(1)}, f32[2,448,128]{2,1,0:T(8,128)}, u32[]{:S(2)}) copy-start(f32[2,448,128]{2,1,0:T(8,128)} %param.4) | copy-start | bytes 1376260
  194.2 329.4 %all-reduce.9.cloned.1.call-start = ((), (), s32[]{:S(2)}) async-start(), calls=%async_computation.2 | async-start | bytes 458752 | tf_op jit(solution)/shard_map/psum | solution.py:42
  426.3 4.8 copy-start.9
  431.2 5.1 copy-start.1
  439.7 318.2 %all-reduce.11.cloned.1.call-start = ((), (), s32[]{:S(2)}) async-start(), calls=%async_computation.3 | async-start | bytes 1966080 | tf_op jit(solution)/shard_map/psum | solution.py:28
  757.9 5.7 copy-start.6
  757.9 5.7 copy-start.10
  757.9 6.1 copy-start.2
  757.9 6.1 copy-start.8
Sparse Core Ops, SparseCore 0:
  9.1 93.3 all-gather.1
  109.4 82.4 all-reduce.6
  194.6 231.7 all-reduce.12
  439.8 83.7 all-reduce.8
  526.2 231.7 all-reduce.10
where the time goes:
time: 775 us
  waiting for transfers between devices  705 us (91%)
  matrix products  50.4 us (7%)
  between operations  13.3 us (2%)
    psum x2, waiting for transfers between devices, row_sums(): lax.psum((transposed_dot(current, vector_rows),) + extra_terms, 'row')  459 us
    psum x2, waiting for transfers between devices, shards(): forward = lax.psum(matmul(current, vcol_now), 'col')  151 us
    all_gather x1, waiting for transfers between devices, shards(): gathered = lax.all_gather(panels, 'row', axis=1, tiled=True)  95.2 us
    dot_general x14, matrix products, matmul(): return jnp.dot(former, latter, precision=lax.Precision.HIGHEST)  20.8 us
    dot_general x4, matrix products, transposed_dot(): lax.dot_general(former, latter, (((0,), (0,)), ((), ())), precision=lax.P...  20.1 us
  transfers between devices with their start and end apart: 5, of which 5 were waited for; matrix products, arithmetic and copies ran while one was open for 3% of the time, Pallas kernels for 0%

commit v1 on v0

--- a/solution.py
+++ b/solution.py
@@ -32,7 +32,9 @@
 def shards(matrix, panels, factors):
     col_index = lax.axis_index("col")
     local_cols = matrix.shape[1]
-    gathered = lax.all_gather(panels, "row", axis=1, tiled=True)
+    gathered = jnp.concatenate(
+        lax.all_to_all(jnp.stack([panels] * lax.axis_size("row")), "row", 0, 0), axis=1
+    )
     vector_cols = lax.dynamic_slice_in_dim(gathered, col_index * local_cols, local_cols, 1)
     current = matrix
     for number in range(panels.shape[0]):

time: 775 us -> 1030 us (1.33)
  waiting for transfers between devices: 705 us -> 923 us
  local copies, waits for them, and re-layouts: 5.37 us -> 30.4 us
  starting transfers between devices: 0.57 us -> 12 us
    all_to_all x0 -> x1, waiting for transfers between devices: none -> 314 us  [shards(): lax.all_to_all(jnp.stack([panels] * lax.axis_size('row')), 'row', 0, 0)]
    all_gather x1 -> x0, waiting for transfers between devices: 95.2 us -> none  [shards(): gathered = lax.all_gather(panels, 'row', axis=1, tiled=True)]
    all_to_all x0 -> x1, local copies, waits for them, and re-layouts: none -> 12.1 us  [shards(): lax.all_to_all(jnp.stack([panels] * lax.axis_size('row')), 'row', 0, 0)]
    all_to_all x0 -> x1, starting transfers between devices: none -> 11.2 us  [shards(): lax.all_to_all(jnp.stack([panels] * lax.axis_size('row')), 'row', 0, 0)]
  transfers between devices with their start and end apart: 5 -> 5, of which waited for: 5 -> 5; matrix products, arithmetic and copies ran while one was open for 3% -> 2% of each run, Pallas kernels for 0% -> 0%
where the time goes in v1:
time: 1030 us
  waiting for transfers between devices  923 us (90%)
  matrix products  49.6 us (5%)
  local copies, waits for them, and re-layouts  30.4 us (3%)
  between operations  13.3 us (1%)
  starting transfers between devices  12 us (1%)
    psum x2, waiting for transfers between devices, row_sums(): lax.psum((transposed_dot(current, vector_rows),) + extra_terms, 'row')  455 us
    all_to_all x1, waiting for transfers between devices, shards(): lax.all_to_all(jnp.stack([panels] * lax.axis_size('row')), 'row', 0, 0)  314 us
    psum x2, waiting for transfers between devices, shards(): forward = lax.psum(matmul(current, vcol_now), 'col')  154 us
  transfers between devices with their start and end apart: 5, of which 5 were waited for; matrix products, arithmetic and copies ran while one was open for 2% of the time, Pallas kernels for 0%

profile of v1, /device:TPU:1, one launch (start us, length us, event | category | flops | bytes accessed | tf_op | source)
XLA Modules:
  0.0 1028.3 jit_solution(12618700984440820401)
XLA Ops:
  6.5 8.0 stack.2
  14.5 11.2 %all-to-all-start = ((f32[32,2,448,128]{3,2,1,0:T(8,128)}), f32[32,2,448,128]{3,2,1,0:T(8,128)}, u32[]{:S(2)}, u32[]{:S(2)}) async-start(f32[32,2,448,128]{3,2,1,0:T(8,128)} %stack.2), calls=%async_computation | async-start | bytes 29360128 | tf_op jit(solution)/shard_map/all_to_all | solution.py:36
  25.7 0.0 all-reduce.7.cloned.1.call-start
  25.7 314.2 %all-to-all-done = f32[32,2,448,128]{3,2,1,0:T(8,128)} async-done(((f32[32,2,448,128]{3,2,1,0:T(8,128)}), f32[32,2,448,128]{3,2,1,0:T(8,128)}, u32[]{:S(2)}, u32[]{:S(2)}) %all-to-all-start) | async-done | bytes 14680096 | tf_op jit(solution)/shard_map/all_to_all | solution.py:36
  340.0 12.1 %copy.4 = f32[32,2,448,128]{3,2,0,1:T(8,128)} copy(f32[32,2,448,128]{3,2,1,0:T(8,128)} %all-to-all-done) | data formatting | bytes 29360128 | tf_op jit(solution)/shard_map/all_to_all | solution.py:36
  352.0 0.0 copy-start
  352.1 2.6 constant_dynamic-slice_fusion.1
  354.7 0.0 copy-start.2
  354.7 0.9 copy-done.2
  355.6 0.0 copy-done
  355.6 3.4 convolution_bitcast_fusion
  359.0 0.0 all-reduce.7.cloned.1.call-update
  359.0 0.2 all-reduce.13.cloned.1.call-start
  359.2 7.8 fusion.49
  367.0 0.0 copy-start.8
  367.0 77.9 %all-reduce.7.cloned.1.call-done = f32[448,128]{1,0:T(8,128)} async-done(((f32[448,128]{1,0:T(8,128)}), f32[448,128]{1,0:T(8,128)}) %all-reduce.7.cloned.1.call-update) | async-done | bytes 229392 | tf_op jit(solution)/shard_map/psum | solution.py:44
  445.0 0.0 copy-start.10
  445.0 2.3 convolution_bitcast_fusion.2
  447.3 0.0 copy-start.3
  447.3 0.0 all-reduce.13.cloned.1.call-update
  447.3 0.3 all-reduce.9.cloned.1.call-start
  447.6 1.9 slice_bitcast_fusion
  449.4 2.4 copy.7
  451.9 0.0 copy-done.8
  451.9 0.0 copy-done.10
  451.9 0.0 copy-start.4
  451.9 0.3 fusion.37
  452.2 227.2 %all-reduce.13.cloned.1.call-done = (f32[1792,128]{1,0:T(8,128)}, f32[128,128]{0,1:T(8,128)}) async-done(((f32[1792,128]{1,0:T(8,128)}, f32[128,128]{0,1:T(8,128)}), (f32[1792,128]{1,0:T(8,128)}, f32[128,128]{0,1:T(8,128)})) %all-reduce.13.cloned.1.call-update) | async-done | bytes 983056 | tf_op jit(solution)/shard_map/psum | solution.py:28
  679.4 0.0 copy-start.7
  679.4 2.2 fusion.31
  681.6 1.1 fusion.35
  682.8 0.3 fusion.33
  683.1 0.0 copy-done.3
  683.1 0.9 fusion.1
  684.0 0.0 copy-done.4
  684.0 0.4 fusion.11
  684.4 0.0 copy-done.7
  684.4 0.0 copy-start.1
  684.4 4.9 convolution_subtract_fusion.1
  689.3 0.0 copy-done.1
  689.3 3.4 fusion.13
  692.7 0.0 all-reduce.9.cloned.1.call-update
  692.7 0.3 all-reduce.11.cloned.1.call-start
  693.0 7.8 fusion.50
  700.8 76.0 %all-reduce.9.cloned.1.call-done = f32[448,128]{1,0:T(8,128)} async-done(((f32[448,128]{1,0:T(8,128)}), f32[448,128]{1,0:T(8,128)}) %all-reduce.9.cloned.1.call-update) | async-done | bytes 229392 | tf_op jit(solution)/shard_map/psum | solution.py:44
  776.8 2.3 convolution_bitcast_fusion.1
  779.0 0.0 all-reduce.11.cloned.1.call-update
  779.1 2.4 copy.8
  781.5 2.0 fusion.29
  783.5 227.6 %all-reduce.11.cloned.1.call-done = (f32[1792,128]{1,0:T(8,128)}, f32[128,128]{0,1:T(8,128)}) async-done(((f32[1792,128]{1,0:T(8,128)}, f32[128,128]{0,1:T(8,128)}), (f32[1792,128]{1,0:T(8,128)}, f32[128,128]{0,1:T(8,128)})) %all-reduce.11.cloned.1.call-update) | async-done | bytes 983056 | tf_op jit(solution)/shard_map/psum | solution.py:28
  1011.1 0.0 copy-start.5
  1011.1 0.0 copy-start.11
  1011.1 0.0 copy-start.6
  1011.1 0.0 copy-start.9
  1011.1 2.3 fusion.23
  1013.4 1.1 fusion.27
  1014.5 0.3 fusion.25
  1014.8 2.1 fusion
  1016.9 0.0 copy-done.5
  1016.9 0.0 copy-done.11
  1016.9 0.4 fusion.9
  1017.3 0.0 copy-done.6
  1017.3 0.0 copy-done.9
  1017.3 4.4 convolution_subtract_fusion
Async XLA Ops:
  14.5 325.5 %all-to-all-start = ((f32[32,2,448,128]{3,2,1,0:T(8,128)}), f32[32,2,448,128]{3,2,1,0:T(8,128)}, u32[]{:S(2)}, u32[]{:S(2)}) async-start(f32[32,2,448,128]{3,2,1,0:T(8,128)} %stack.2), calls=%async_computation | async-start | bytes 29360128 | tf_op jit(solution)/shard_map/all_to_all | solution.py:36
  25.7 419.3 %all-reduce.7.cloned.1.call-start = ((), (), s32[]{:S(2)}) async-start(), calls=%async_computation.1 | async-start | bytes 458752 | tf_op jit(solution)/shard_map/psum | solution.py:44
  352.0 3.6 copy-start
  354.7 0.9 copy-start.2
  359.0 320.4 %all-reduce.13.cloned.1.call-start = ((), (), s32[]{:S(2)}) async-start(), calls=%async_computation.4 | async-start | bytes 1966080 | tf_op jit(solution)/shard_map/psum | solution.py:28
  367.0 84.8 %copy-start.8 = (f32[2,128,128]{2,1,0:T(8,128)S(1)}, f32[2,128,128]{2,1,0:T(8,128)}, u32[]{:S(2)}) copy-start(f32[2,128,128]{2,1,0:T(8,128)} %param.5) | copy-start | bytes 393220
  445.0 6.9 copy-start.10
  447.3 235.8 %copy-start.3 = (f32[1,1792,128]{2,1,0:T(8,128)S(1)}, f32[1,1792,128]{2,1,0:T(8,128)}, u32[]{:S(2)}) copy-start(f32[1,1792,128]{2,1,0:T(8,128)} %copy-done.2) | copy-start | bytes 2752516
  447.3 329.5 %all-reduce.9.cloned.1.call-start = ((), (), s32[]{:S(2)}) async-start(), calls=%async_computation.2 | async-start | bytes 458752 | tf_op jit(solution)/shard_map/psum | solution.py:44
  451.9 232.2 %copy-start.4 = (f32[2,448,128]{2,1,0:T(8,128)S(1)}, f32[2,448,128]{2,1,0:T(8,128)}, u32[]{:S(2)}) copy-start(f32[2,448,128]{2,1,0:T(8,128)} %param.4) | copy-start | bytes 1376260
  679.4 5.0 copy-start.7
  684.4 4.9 copy-start.1
  692.7 318.4 %all-reduce.11.cloned.1.call-start = ((), (), s32[]{:S(2)}) async-start(), calls=%async_computation.3 | async-start | bytes 1966080 | tf_op jit(solution)/shard_map/psum | solution.py:28
  1011.1 5.8 copy-start.5
  1011.1 5.8 copy-start.11
  1011.1 6.2 copy-start.6
  1011.1 6.2 copy-start.9
Sparse Core Ops, SparseCore 0:
  359.1 85.7 all-reduce.6
  447.7 231.7 all-reduce.12
  692.8 83.8 all-reduce.8
  779.3 231.7 all-reduce.10

commit v2 on v0

--- a/solution.py
+++ b/solution.py
@@ -39,7 +39,7 @@
         vector_rows = panels[number]
         vcol_now = vector_cols[number]
         factor = factors[number]
-        forward = lax.psum(matmul(current, vcol_now), "col")
+        forward = jnp.sum(lax.all_gather(matmul(current, vcol_now), "col"), axis=0)
         forward_cols, summed = row_sums(
             current, vector_rows, (transposed_dot(vector_rows, forward),)
         )

time: 775 us -> 718 us (0.926)
  waiting for transfers between devices: 705 us -> 646 us
    psum x2 -> x0, waiting for transfers between devices: 151 us -> none  [shards(): forward = lax.psum(matmul(current, vcol_now), 'col')]
    all_gather x0 -> x2, waiting for transfers between devices: none -> 100 us  [shards(): forward = jnp.sum(lax.all_gather(matmul(current, vcol_now), 'col'), axis=0)]
    psum x2, waiting for transfers between devices: 459 us -> 450 us  [row_sums(): lax.psum((transposed_dot(current, vector_rows),) + extra_terms, 'row')]
where the time goes in v2:
time: 718 us; the launch traced here: 717 us
  waiting for transfers between devices  646 us (90%)
  matrix products  49.3 us (7%)
  between operations  13.3 us (2%)
    psum x2, waiting for transfers between devices, row_sums(): lax.psum((transposed_dot(current, vector_rows),) + extra_terms, 'row')  450 us
    all_gather x2, waiting for transfers between devices, shards(): forward = jnp.sum(lax.all_gather(matmul(current, vcol_now), 'col'), axis=0)  100 us
    all_gather x1, waiting for transfers between devices, shards(): gathered = lax.all_gather(panels, 'row', axis=1, tiled=True)  95.2 us
    dot_general x4, matrix products, transposed_dot(): lax.dot_general(former, latter, (((0,), (0,)), ((), ())), precision=lax.P...  19.9 us
    dot_general x14, matrix products, matmul(): return jnp.dot(former, latter, precision=lax.Precision.HIGHEST)  19.8 us
  transfers between devices with their start and end apart: 5, of which 5 were waited for; matrix products, arithmetic and copies ran while one was open for 3% of the time, Pallas kernels for 0%

profile of v2, /device:TPU:1, one launch (start us, length us, event | category | flops | bytes accessed | tf_op | source)
XLA Modules:
  0.0 717.4 jit_solution(3361767524532197473)
XLA Ops:
  6.5 0.0 copy-start
  6.5 0.0 all-gather.6.cloned.1.call-start
  6.5 0.7 all-gather.6.cloned.1.call-update
  7.3 0.0 all-gather.8.cloned.1.call-start
  7.3 95.2 %all-gather.6.cloned.1.call-done = f32[2,14336,128]{2,1,0:T(8,128)} async-done(((f32[2,448,128]{2,1,0:T(8,128)}), f32[2,14336,128]{2,1,0:T(8,128)}) %all-gather.6.cloned.1.call-update) | async-done | bytes 14680080 | tf_op jit(solution)/shard_map/all_gather | solution.py:35
  102.5 2.5 dynamic-slice_bitcast_fusion
  105.0 0.0 copy-start.3
  105.0 0.9 copy-done.3
  105.9 0.0 copy-done
  105.9 3.4 convolution_bitcast_fusion
  109.3 0.0 all-gather.8.cloned.1.call-update
  109.3 0.0 all-reduce.7.cloned.1.call-start
  109.4 7.8 %fusion.44 = f32[1792,128]{1,0:T(8,128)} fusion(f32[448,1792]{1,0:T(8,128)S(1)} %copy-done, f32[2,448,128]{2,1,0:T(8,128)} %param.4), kind=kOutput, calls=%fused_computation.57 | convolution fusion | flops 1233125376 | bytes 4358144 | tf_op jit(solution)/shard_map/dot_general | solution.py:12
  117.1 0.0 copy-start.5
  117.1 0.0 copy-start.7
  117.1 49.3 %all-gather.8.cloned.1.call-done = f32[3584,128]{1,0:T(8,128)} async-done(((f32[448,128]{1,0:T(8,128)}), f32[3584,128]{1,0:T(8,128)}) %all-gather.8.cloned.1.call-update) | async-done | bytes 1835024 | tf_op jit(solution)/shard_map/all_gather | solution.py:42
  166.4 0.0 copy-start.4
  166.4 1.7 reduce_sum.18
  168.1 2.2 convolution_bitcast_fusion.2
  170.3 0.0 all-reduce.7.cloned.1.call-update
  170.3 0.2 all-gather.10.cloned.1.call-start
  170.5 0.0 copy-done.5
  170.6 0.8 slice_bitcast_fusion
  171.4 0.0 copy-done.7
  171.4 0.3 fusion.32
  171.7 225.3 %all-reduce.7.cloned.1.call-done = (f32[1792,128]{1,0:T(8,128)}, f32[128,128]{0,1:T(8,128)}) async-done(((f32[1792,128]{1,0:T(8,128)}, f32[128,128]{0,1:T(8,128)}), (f32[1792,128]{1,0:T(8,128)}, f32[128,128]{0,1:T(8,128)})) %all-reduce.7.cloned.1.call-update) | async-done | bytes 983056 | tf_op jit(solution)/shard_map/psum | solution.py:28
  397.0 0.0 copy-start.9
  397.0 2.1 fusion.26
  399.1 1.1 fusion.30
  400.2 0.3 fusion.28
  400.5 0.0 copy-done.4
  400.5 0.9 fusion.1
  401.5 0.4 fusion.11
  401.8 0.0 copy-done.9
  401.8 0.0 copy-start.1
  401.8 5.1 convolution_subtract_fusion.1
  406.9 0.0 copy-done.1
  406.9 3.4 fusion.46
  410.3 0.0 all-gather.10.cloned.1.call-update
  410.3 0.3 all-reduce.5.cloned.1.call-start
  410.6 7.8 %fusion.45 = f32[1792,128]{1,0:T(8,128)} fusion(f32[448,1792]{1,0:T(8,128)S(1)} %convolution_subtract_fusion.1, f32[2,448,128]{2,1,0:T(8,128)} %param.4), kind=kOutput, calls=%fused_computation.58 | convolution fusion | flops 1233125376 | bytes 4358144 | tf_op jit(solution)/shard_map/dot_general | solution.py:12
  418.4 50.7 %all-gather.10.cloned.1.call-done = f32[3584,128]{1,0:T(8,128)} async-done(((f32[448,128]{1,0:T(8,128)}), f32[3584,128]{1,0:T(8,128)}) %all-gather.10.cloned.1.call-update) | async-done | bytes 1835024 | tf_op jit(solution)/shard_map/all_gather | solution.py:42
  469.0 2.3 reduce_sum.19
  471.3 2.3 convolution_bitcast_fusion.1
  473.6 0.0 all-reduce.5.cloned.1.call-update
  473.6 2.0 fusion.24
  475.6 224.7 %all-reduce.5.cloned.1.call-done = (f32[1792,128]{1,0:T(8,128)}, f32[128,128]{0,1:T(8,128)}) async-done(((f32[1792,128]{1,0:T(8,128)}, f32[128,128]{0,1:T(8,128)}), (f32[1792,128]{1,0:T(8,128)}, f32[128,128]{0,1:T(8,128)})) %all-reduce.5.cloned.1.call-update) | async-done | bytes 983056 | tf_op jit(solution)/shard_map/psum | solution.py:28
  700.3 0.0 copy-start.6
  700.3 0.0 copy-start.10
  700.3 0.0 copy-start.2
  700.3 0.0 copy-start.8
  700.3 2.2 fusion.18
  702.5 1.1 fusion.22
  703.6 0.3 fusion.20
  703.9 2.1 fusion
  706.0 0.0 copy-done.6
  706.0 0.0 copy-done.10
  706.0 0.4 fusion.9
  706.4 0.0 copy-done.2
  706.4 0.0 copy-done.8
  706.4 4.5 convolution_subtract_fusion
Async XLA Ops:
  6.5 99.4 %copy-start = (f32[448,1792]{1,0:T(8,128)S(1)}, f32[448,1792]{1,0:T(8,128)}, u32[]{:S(2)}) copy-start(f32[448,1792]{1,0:T(8,128)} %param.3) | copy-start | bytes 9633796
  6.5 96.0 %all-gather.6.cloned.1.call-start = ((), (), s32[]{:S(2)}) async-start(), calls=%async_computation | async-start | bytes 15138816 | tf_op jit(solution)/shard_map/all_gather | solution.py:35
  7.3 159.2 %all-gather.8.cloned.1.call-start = ((), (), s32[]{:S(2)}) async-start(), calls=%async_computation.1 | async-start | bytes 2064384 | tf_op jit(solution)/shard_map/all_gather | solution.py:42
  105.0 0.9 copy-start.3
  109.3 287.7 %all-reduce.7.cloned.1.call-start = ((), (), s32[]{:S(2)}) async-start(), calls=%async_computation.4 | async-start | bytes 1966080 | tf_op jit(solution)/shard_map/psum | solution.py:28
  117.1 53.4 %copy-start.5 = (f32[2,448,128]{2,1,0:T(8,128)S(1)}, f32[2,448,128]{2,1,0:T(8,128)}, u32[]{:S(2)}) copy-start(f32[2,448,128]{2,1,0:T(8,128)} %param.4) | copy-start | bytes 1376260
  117.1 54.2 %copy-start.7 = (f32[2,128,128]{2,1,0:T(8,128)S(1)}, f32[2,128,128]{2,1,0:T(8,128)}, u32[]{:S(2)}) copy-start(f32[2,128,128]{2,1,0:T(8,128)} %param.5) | copy-start | bytes 393220
  166.4 234.1 %copy-start.4 = (f32[1792,128]{1,0:T(8,128)S(1)}, f32[1792,128]{1,0:T(8,128)}, u32[]{:S(2)}) copy-start(f32[1792,128]{1,0:T(8,128)} %copy-done.3) | copy-start | bytes 2752516
  170.3 298.7 %all-gather.10.cloned.1.call-start = ((), (), s32[]{:S(2)}) async-start(), calls=%async_computation.2 | async-start | bytes 2064384 | tf_op jit(solution)/shard_map/all_gather | solution.py:42
  397.0 4.8 copy-start.9
  401.8 5.1 copy-start.1
  410.3 290.0 %all-reduce.5.cloned.1.call-start = ((), (), s32[]{:S(2)}) async-start(), calls=%async_computation.3 | async-start | bytes 1966080 | tf_op jit(solution)/shard_map/psum | solution.py:28
  700.3 5.7 copy-start.6
  700.3 5.7 copy-start.10
  700.3 6.1 copy-start.2
  700.3 6.1 copy-start.8
Sparse Core Ops, SparseCore 0:
  9.1 93.3 all-gather.5
  109.4 56.9 all-gather.7
  170.4 226.5 all-reduce.6
  410.5 58.5 all-gather.9
  473.7 226.5 all-reduce.4
